TPU v7x, 512 devices: a whole 4x8x8 slice. The times are simulated.
512 devices in a mesh: ta: 8 (over z), gx: 64 (over x, y, core).
Axes of the slice: x: 4, y: 8, z: 8, core: 2. Of those that a mesh axis runs over, the one named last changes fastest.
Arguments:
- gauge_links: float32 [3, 2, 3, 3, 512, 9216], P(None, None, None, None, ('ta', 'gx')), parts along dimension 4, may hold values from -1 to 1, as said below
Outputs:
- fixed_links: float32 [3, 2, 3, 3, 512, 9216], P(None, None, None, None, ('ta', 'gx')), parts along dimension 4
- drift_values: float32 [8], P('ta'), parts along dimension 0
There are 8 independent parts, one for each index of `ta`. A program takes and returns all parts, laid end to end along the dimension named above; each array names one. Nothing has to cross between parts.
Inputs may be any that keep to these rules, and one draw needn't show every extreme that they name: `gauge_links`: for every direction and site the complex matrix is unitary.
All inputs are finite; a program needn't handle non-finite values.
Results may differ from a plain program's by a relative error of at most 0.0003.
Values sent between devices are 32-bit elements; how exact they have to be, the bound alone decides.
A program may use at most 128 MiB of HBM per device.

v0:
```python
import math

import jax
import jax.numpy as jnp
import numpy as np
from jax import lax
from jax.experimental import pallas as pl
from jax.experimental.pallas import tpu as pltpu
from jax.sharding import PartitionSpec as P

SIDE = 96
NX = 64
CELLS = SIDE * SIDE
ROWS, LANES = 24, 384
STEP_SIZE = 0.08
PEAK_SQUARE = 12.0
MESH = pl.DeviceIdType.MESH
F32 = jnp.float32
BF16 = jnp.bfloat16


def cas(length):
    index = np.arange(length)
    angle = 2.0 * np.pi * ((index[:, None] * index[None, :]) % length) / length
    return np.cos(angle) + np.sin(angle)


def sine_square(length):
    return 4.0 * np.sin(np.pi * np.arange(length) / length) ** 2


def halves(table):
    table = np.asarray(table, np.float32)
    high = table.astype(BF16)
    low = (table - high.astype(np.float32)).astype(BF16)
    return np.stack([high, low])


def make_tables():
    side = cas(SIDE)
    spread = np.zeros((LANES, 512))
    for k in range(4):
        spread[96 * k : 96 * k + 96, 128 * k : 128 * k + 96] = side
    order = np.array([4 * h + k for k in range(4) for h in range(ROWS)])
    down = side[:, order]
    square = sine_square(SIDE)
    plane = np.zeros((NX, 9, 128), np.float32)
    lane = np.arange(128)
    for owner in range(NX):
        for i in range(9):
            tile = 9 * (owner // 8) + i
            row = (tile // 6) * 8 + owner % 8
            part = tile % 3
            column = np.where(lane < 96, lane, 32 * part + lane - 96)
            plane[owner, i] = square[row] + square[column]
    along = np.broadcast_to(sine_square(NX)[:, None], (NX, 128)).astype(np.float32)
    return (
        halves(spread),
        halves(spread.T),
        halves(down),
        halves(down.T),
        halves(cas(NX)),
        plane,
        np.ascontiguousarray(along),
    )


def split(x):
    high = x.astype(BF16)
    return high, (x - high.astype(F32)).astype(BF16)


def dot(a, b):
    return jnp.dot(a, b, preferred_element_type=F32)


def data_times(x, table):
    high, low = split(x)
    return dot(high, table[0]) + (dot(low, table[0]) + dot(high, table[1]))


def times_data(table, x):
    high, low = split(x)
    return dot(table[0], high) + (dot(table[0], low) + dot(table[1], high))


def projected(get):
    im0, im1, im2 = get(1, 0, 0), get(1, 1, 1), get(1, 2, 2)
    third = (im0 + im1 + im2) * (1.0 / 3.0)
    out = [im0 - third, im1 - third]
    for i, j in ((0, 1), (0, 2), (1, 2)):
        out.append(0.5 * (get(0, i, j) - get(0, j, i)))
        out.append(0.5 * (get(1, i, j) + get(1, j, i)))
    return out


def cayley(a):
    h0, h1, q01, p01, q02, p02, q12, p12 = a
    h2 = -(h0 + h1)
    s01 = p01 * p01 + q01 * q01
    s02 = p02 * p02 + q02 * q02
    s12 = p12 * p12 + q12 * q12
    t0, t1, t2 = h0 * h0, h1 * h1, h2 * h2
    plus = 1.0 + (0.5 * (t0 + t1 + t2) + (s01 + s02 + s12))
    mr = p01 * p12 - q01 * q12
    mi = -(p01 * q12 + q01 * p12)
    nr = p02 * p12 + q02 * q12
    ni = p02 * q12 - q02 * p12
    kr = p01 * p02 + q01 * q02
    ki = q01 * p02 - p01 * q02
    delta = h0 * h1 * h2 + 2.0 * (mr * p02 - mi * q02) - (h0 * s12 + h1 * s02 + h2 * s01)
    scale = 2.0 / (plus * plus + delta * delta)
    u = plus * scale
    v = -delta * scale
    real = [[None] * 3 for _ in range(3)]
    imag = [[None] * 3 for _ in range(3)]
    for i, (h, b) in enumerate(
        (
            (h0, plus - (t0 + s01 + s02)),
            (h1, plus - (t1 + s01 + s12)),
            (h2, plus - (t2 + s02 + s12)),
        )
    ):
        real[i][i] = u * b - v * h - 1.0
        imag[i][i] = u * h + v * b
    for i, j, p, q, br, bi in (
        (0, 1, p01, q01, h2 * p01 - nr, -h2 * q01 - ni),
        (0, 2, p02, q02, h1 * p02 - mr, -h1 * q02 - mi),
        (1, 2, p12, q12, h0 * p12 - kr, -h0 * q12 - ki),
    ):
        ur, ui = br + q, bi + p
        lr, li = br - q, p - bi
        real[i][j] = u * ur - v * ui
        imag[i][j] = u * ui + v * ur
        real[j][i] = u * lr - v * li
        imag[j][i] = u * li + v * lr
    return [real[i][j] for i in range(3) for j in range(3)] + [imag[i][j] for i in range(3) for j in range(3)]


def moved(g, u, ahead):
    tr, ti = [], []
    for i in range(3):
        for j in range(3):
            r = m = None
            for k in range(3):
                ar, ai = g[3 * i + k], g[9 + 3 * i + k]
                br, bi = u[3 * k + j], u[9 + 3 * k + j]
                x, y = ar * br - ai * bi, ar * bi + ai * br
                r, m = (x, y) if r is None else (r + x, m + y)
            tr.append(r)
            ti.append(m)
    out_r, out_i = [], []
    for i in range(3):
        for j in range(3):
            r = m = None
            for k in range(3):
                ar, ai = tr[3 * i + k], ti[3 * i + k]
                br, bi = ahead[3 * j + k], ahead[9 + 3 * j + k]
                x, y = ar * br + ai * bi, ai * br - ar * bi
                r, m = (x, y) if r is None else (r + x, m + y)
            out_r.append(r)
            out_i.append(m)
    return out_r + out_i


def forward_modes(fields, spread, down, tiles_ref):
    part = data_times(fields, spread)
    stacked = jnp.concatenate(
        [
            jnp.concatenate([part[24 * f : 24 * f + 24, 128 * k : 128 * k + 128] for f in range(8)], axis=1)
            for k in range(4)
        ],
        axis=0,
    )
    modes = times_data(down, stacked)
    lane = lax.broadcasted_iota(jnp.int32, (SIDE, 128), 1)
    for q in range(2):
        last = modes[:, 128 * (4 * q + 3) : 128 * (4 * q + 4)]
        for j in range(3):
            own = modes[:, 128 * (4 * q + j) : 128 * (4 * q + j + 1)]
            shift = 96 - 32 * j
            tile = jnp.where(lane < 96, own, pltpu.roll(last, shift, 1))
            for b in range(12):
                tiles_ref[6 * b + 3 * q + j] = tile[8 * b : 8 * b + 8]


def inverse_fields(tiles_ref, spread_t, down_t):
    lane = lax.broadcasted_iota(jnp.int32, (SIDE, 128), 1)
    blocks = []
    for q in range(2):
        tiles = [
            jnp.concatenate([tiles_ref[6 * b + 3 * q + j] for b in range(12)], axis=0) for j in range(3)
        ]
        rolled = [pltpu.roll(tiles[j], 32 * j + 32, 1) for j in range(3)]
        last = jnp.where(lane < 32, rolled[0], jnp.where(lane < 64, rolled[1], rolled[2]))
        blocks += tiles + [last]
    stacked = times_data(down_t, jnp.concatenate(blocks, axis=1))
    part = jnp.concatenate(
        [
            jnp.concatenate([stacked[24 * k : 24 * k + 24, 128 * f : 128 * f + 128] for k in range(4)], axis=1)
            for f in range(8)
        ],
        axis=0,
    )
    return data_times(part, spread_t)


def row_turned(x, shift):
    count = x.shape[0] // ROWS
    return pltpu.roll(x.reshape(count, ROWS, x.shape[1]), shift, 1).reshape(x.shape)


def lane_of(x):
    return lax.broadcasted_iota(jnp.int32, x.shape, 1)


def from_y_before(x):
    turned = pltpu.roll(x, 96, 1)
    return jnp.where(lane_of(x) < 96, row_turned(turned, 1), turned)


def from_z_before(x):
    return jnp.where(lane_of(x) % 96 == 0, pltpu.roll(x, LANES - 95, 1), pltpu.roll(x, 1, 1))


def from_y_after(x):
    turned = pltpu.roll(x, LANES - 96, 1)
    return jnp.where(lane_of(x) >= 288, row_turned(turned, ROWS - 1), turned)


def from_z_after(x):
    return jnp.where(lane_of(x) % 96 == 95, pltpu.roll(x, 95, 1), pltpu.roll(x, LANES - 1, 1))


def kernel(
    u_hbm, spread_hbm, spread_t_hbm, down, down_t, along, plane_hbm, square_x,
    out_hbm, drift_ref,
    u, spread, spread_t, plane, own, prev, rest, snd, rcv, sol, back, ahead, part, parts,
    g, gy, gz, gx, act,
    local_sem, edge_sem, out_send, out_recv, back_send, back_recv, part_send, part_recv,
):
    me = lax.axis_index("gx")
    after, before = lax.rem(me + 1, NX), lax.rem(me + NX - 1, NX)

    loads = [
        pltpu.make_async_copy(u_hbm.at[pl.ds(18 * d, 18)], u.at[pl.ds(18 * d, 18)], local_sem.at[d])
        for d in range(3)
    ]
    loads.append(pltpu.make_async_copy(spread_hbm, spread, local_sem.at[3]))
    loads.append(pltpu.make_async_copy(spread_t_hbm, spread_t, local_sem.at[4]))
    loads.append(pltpu.make_async_copy(plane_hbm.at[me], plane, local_sem.at[5]))
    for load in loads:
        load.start()

    barrier = pltpu.get_barrier_semaphore()

    def greet(k, carry):
        peer = lax.rem(me + k, NX)
        pl.semaphore_signal(barrier, inc=1, device_id={"gx": peer}, device_id_type=MESH)
        return carry

    lax.fori_loop(1, NX, greet, 0)

    def project(d, into):
        for j in range(3):
            fields = projected(
                lambda p, a, b: u[18 * d + 9 * p + 3 * a + b, pl.ds(j, ROWS, stride=3), :]
            )
            for f in range(8):
                into[pl.ds(ROWS * f, ROWS), pl.ds(128 * j, 128)] = fields[f]

    loads[0].wait()
    project(0, own)
    pl.semaphore_wait(barrier, NX - 1)

    edge = pltpu.make_async_remote_copy(
        src_ref=own, dst_ref=prev, send_sem=edge_sem.at[0], recv_sem=edge_sem.at[1],
        device_id={"gx": after}, device_id_type=MESH,
    )
    edge.start()

    loads[1].wait()
    project(1, act)
    middle = act[...]
    rest[...] = from_y_before(middle) - middle - own[...]
    loads[2].wait()
    project(2, act)
    middle = act[...]
    rest[...] += from_z_before(middle) - middle
    loads[3].wait()
    loads[4].wait()
    loads[5].wait()

    edge.wait()
    fields = rest[...] + prev[...]
    f0, f1, tail = fields[:24], fields[24:48], fields[48:]
    both = f0 + f1
    square = f0 * f0 + f1 * f1 + both * both
    total = jnp.sum(square, axis=0, keepdims=True) + 2.0 * jnp.sum(tail * tail, axis=0, keepdims=True)
    total = total[:, :128] + total[:, 128:256] + total[:, 256:]
    part[...] = jnp.broadcast_to(total, (8, 128))
    forward_modes(fields, spread, down, snd)

    group, line = me // 8, lax.rem(me, 8)

    def there(peer):
        return pltpu.make_async_remote_copy(
            src_ref=snd.at[pl.ds(9 * (peer // 8), 9), lax.rem(peer, 8)], dst_ref=rcv.at[:, me],
            send_sem=out_send.at[peer], recv_sem=out_recv.at[me],
            device_id={"gx": peer}, device_id_type=MESH,
        )

    def there_from(peer):
        return pltpu.make_async_remote_copy(
            src_ref=snd.at[pl.ds(9 * (peer // 8), 9), lax.rem(peer, 8)], dst_ref=rcv.at[:, peer],
            send_sem=out_send.at[peer], recv_sem=out_recv.at[peer],
            device_id={"gx": peer}, device_id_type=MESH,
        )

    def home(peer):
        return pltpu.make_async_remote_copy(
            src_ref=sol.at[:, peer], dst_ref=back.at[pl.ds(9 * group, 9), line],
            send_sem=back_send.at[peer], recv_sem=back_recv.at[me],
            device_id={"gx": peer}, device_id_type=MESH,
        )

    def home_from(peer):
        return pltpu.make_async_remote_copy(
            src_ref=sol.at[:, peer], dst_ref=back.at[pl.ds(9 * (peer // 8), 9), lax.rem(peer, 8)],
            send_sem=back_send.at[peer], recv_sem=back_recv.at[peer],
            device_id={"gx": peer}, device_id_type=MESH,
        )

    def shared(peer):
        return pltpu.make_async_remote_copy(
            src_ref=part.at[0], dst_ref=parts.at[me],
            send_sem=part_send.at[peer], recv_sem=part_recv.at[me],
            device_id={"gx": peer}, device_id_type=MESH,
        )

    def shared_from(peer):
        return pltpu.make_async_remote_copy(
            src_ref=part.at[0], dst_ref=parts.at[peer],
            send_sem=part_send.at[peer], recv_sem=part_recv.at[peer],
            device_id={"gx": peer}, device_id_type=MESH,
        )

    def each(action, sign):
        def body(k, carry):
            action(lax.rem(me + NX + sign * k, NX))
            return carry

        lax.fori_loop(1, NX, body, 0)

    each(lambda peer: there(peer).start(), 1)
    mine = pltpu.make_async_copy(snd.at[pl.ds(9 * group, 9), line], rcv.at[:, me], local_sem.at[0])
    mine.start()
    each(lambda peer: shared(peer).start(), 1)
    own_part = pltpu.make_async_copy(part.at[0], parts.at[me], local_sem.at[1])
    own_part.start()

    factor = PEAK_SQUARE * STEP_SIZE * 0.5 / (NX * CELLS)
    filters = []
    for i in range(9):
        square = square_x[...] + plane[pl.ds(i, 1), :]
        positive = square > 0.0
        filters.append(jnp.where(positive, factor / jnp.where(positive, square, 1.0), 0.0))
    filters = jnp.concatenate(filters, axis=1)

    mine.wait()
    each(lambda peer: there_from(peer).wait(), -1)

    waves = times_data(along, jnp.concatenate([rcv[i] for i in range(9)], axis=1))
    waves = times_data(along, waves * filters)
    for i in range(9):
        sol[i] = waves[:, 128 * i : 128 * i + 128]

    each(lambda peer: home(peer).start(), 1)
    mine = pltpu.make_async_copy(sol.at[:, me], back.at[pl.ds(9 * group, 9), line], local_sem.at[0])
    mine.start()

    own_part.wait()
    each(lambda peer: shared_from(peer).wait(), -1)
    drift_ref[0] = jnp.sum(parts[...]) * (1.0 / (9.0 * NX * CELLS))

    mine.wait()
    each(lambda peer: home_from(peer).wait(), -1)

    onward = pltpu.make_async_remote_copy(
        src_ref=back, dst_ref=ahead, send_sem=edge_sem.at[2], recv_sem=edge_sem.at[3],
        device_id={"gx": before}, device_id_type=MESH,
    )
    onward.start()

    def rotate(tiles, into):
        act[...] = inverse_fields(tiles, spread_t, down_t)

        def body(c, carry):
            r, j = pl.multiple_of(8 * (c // 3), 8), pl.multiple_of(128 * (c % 3), 128)
            entries = cayley([act[pl.ds(ROWS * f + r, 8), pl.ds(j, 128)] for f in range(8)])
            for e in range(18):
                into[pl.ds(ROWS * e + r, 8), pl.ds(j, 128)] = entries[e]
            return carry

        lax.fori_loop(0, 9, body, 0)

    rotate(back, g)
    whole = g[...]
    gy[...] = from_y_after(whole)
    gz[...] = from_z_after(whole)

    stores = []

    def update(d, aheads):
        def body(c, carry):
            i, t = c // 3, c % 3
            r, j = pl.multiple_of(8 * i, 8), pl.multiple_of(128 * t, 128)
            read = lambda ref: [ref[pl.ds(ROWS * e + r, 8), pl.ds(j, 128)] for e in range(18)]
            links = [u[18 * d + e, pl.ds(24 * i + t, 8, stride=3), :] for e in range(18)]
            new = moved(read(g), links, read(aheads))
            for e in range(18):
                u[18 * d + e, pl.ds(24 * i + t, 8, stride=3), :] = new[e]
            return carry

        lax.fori_loop(0, 9, body, 0)
        store = pltpu.make_async_copy(
            u.at[pl.ds(18 * d, 18)], out_hbm.at[pl.ds(18 * d, 18)], local_sem.at[d]
        )
        store.start()
        stores.append(store)

    update(1, gy)
    update(2, gz)
    onward.wait()
    rotate(ahead, gx)
    update(0, gx)
    for store in stores:
        store.wait()


def local(gauge_links):
    tables = make_tables()
    spread, spread_t, down, down_t, along, plane, square_x = (jnp.asarray(t) for t in tables)
    vmem = pl.BlockSpec(memory_space=pltpu.VMEM)
    anywhere = pl.BlockSpec(memory_space=pl.ANY)
    dma = pltpu.SemaphoreType.DMA
    fields = pltpu.VMEM((8 * ROWS, LANES), F32)
    matrix = pltpu.VMEM((18 * ROWS, LANES), F32)
    tiles = pltpu.VMEM((72, 8, 128), F32)
    waves = pltpu.VMEM((9, NX, 128), F32)
    links, drift = pl.pallas_call(
        kernel,
        out_shape=(
            jax.ShapeDtypeStruct((54, 72, 128), F32),
            jax.ShapeDtypeStruct((1,), F32),
        ),
        in_specs=[anywhere, anywhere, anywhere, vmem, vmem, vmem, anywhere, vmem],
        out_specs=(anywhere, pl.BlockSpec(memory_space=pltpu.SMEM)),
        scratch_shapes=[
            pltpu.VMEM((54, 72, 128), F32),
            pltpu.VMEM((2, LANES, 512), BF16),
            pltpu.VMEM((2, 512, LANES), BF16),
            pltpu.VMEM((9, 128), F32),
            fields, fields, fields,
            tiles, waves, waves, tiles, tiles,
            pltpu.VMEM((8, 128), F32),
            pltpu.VMEM((NX, 128), F32),
            matrix, matrix, matrix, matrix,
            fields,
            dma((6,)), dma((4,)),
            dma((NX,)), dma((NX,)), dma((NX,)), dma((NX,)), dma((NX,)), dma((NX,)),
        ],
        compiler_params=pltpu.CompilerParams(collective_id=0, has_side_effects=True),
    )(gauge_links.reshape(54, 72, 128), spread, spread_t, down, down_t, along, plane, square_x)
    return links.reshape(gauge_links.shape), drift


def solution(mesh):
    split_x = ("ta", "gx")
    return jax.shard_map(
        local,
        mesh=mesh,
        in_specs=(P(None, None, None, None, split_x, None),),
        out_specs=(P(None, None, None, None, split_x, None), P("ta")),
        check_vma=False,
    )
```

profile of v0, /device:TPU:1, one launch (start us, length us, event | category | flops | bytes accessed | tf_op | source)
XLA Modules:
  0.0 54.8 jit_solution(18117092454306741434)
XLA Ops:
  0.6 49.4 %shard_map.95 = (f32[54,72,128]{2,1,0:T(8,128)}, f32[1]{0:T(128)}) custom-call(f32[54,72,128]{2,1,0:T(8,128)} %bitcast.2, bf16[2,384,512]{2,1,0:T(8,128)(2,1)} %constant.14.clone.spread_hbm, bf16[2,512,384]{2,1,0:T(8,128)(2,1)} %constant.15.clone.spread_t_hbm, bf16[2,96,96]{2,1,0:T(8,128)(2,1)} %constant.16.clone.down, ...), custom_call_target="tpu_custom_call" | custom-call | tf_op jit(solution)/shard_map/pallas_call | solution.py:451
  50.1 3.0 %copy.14 = f32[3,2,3,3,1,9216]{5,4,3,2,1,0:T(1,128)} copy(f32[3,2,3,3,1,9216]{5,4,3,2,1,0:T(1,128)} %bitcast.3) | data formatting | bytes 3981312
where the time goes:
time: 55 us; the launch traced here: 54.8 us
  Pallas kernels  49.4 us (90%)
  local copies, waits for them, and re-layouts  2.96 us (5%)
  between operations  2.4 us (4%)
    pallas_call x1, Pallas kernels, local(): pl.pallas_call(kernel, out_shape=(jax.ShapeDtypeStruct((54, 72, 128), F32...  49.4 us
    unnamed x1, local copies, waits for them, and re-layouts  2.96 us

commit v1 on v0

v1 whole, which is shorter than its diff:
```python
import math

import jax
import jax.numpy as jnp
import numpy as np
from jax import lax
from jax.experimental import pallas as pl
from jax.experimental.pallas import tpu as pltpu
from jax.sharding import PartitionSpec as P

SIDE = 96
NX = 64
CELLS = SIDE * SIDE
ROWS, LANES = 24, 384
STEP_SIZE = 0.08
PEAK_SQUARE = 12.0
MESH = pl.DeviceIdType.MESH
F32 = jnp.float32
BF16 = jnp.bfloat16


def cas(length):
    index = np.arange(length)
    angle = 2.0 * np.pi * ((index[:, None] * index[None, :]) % length) / length
    return np.cos(angle) + np.sin(angle)


def sine_square(length):
    return 4.0 * np.sin(np.pi * np.arange(length) / length) ** 2


def halves(table):
    table = np.asarray(table, np.float32)
    high = table.astype(BF16)
    low = (table - high.astype(np.float32)).astype(BF16)
    return np.stack([high, low])


def make_tables():
    side = cas(SIDE)
    spread = np.zeros((LANES, 512))
    for k in range(4):
        spread[96 * k : 96 * k + 96, 128 * k : 128 * k + 96] = side
    order = np.array([4 * h + k for k in range(4) for h in range(ROWS)])
    down = side[:, order]
    square = sine_square(SIDE)
    plane = np.zeros((NX, 9, 128), np.float32)
    lane = np.arange(128)
    for owner in range(NX):
        for i in range(9):
            tile = 9 * (owner // 16) + i
            row = (tile // 3) * 8 + (owner // 2) % 8
            part = tile % 3
            column = np.where(lane < 96, lane, 32 * part + lane - 96)
            plane[owner, i] = square[row] + square[column]
    along = np.broadcast_to(sine_square(NX)[:, None], (NX, 128)).astype(np.float32)
    return (
        halves(spread),
        halves(spread.T),
        halves(down),
        halves(down.T),
        halves(cas(NX)),
        plane,
        np.ascontiguousarray(along),
    )


def split(x):
    high = x.astype(BF16)
    return high, (x - high.astype(F32)).astype(BF16)


def dot(a, b):
    return jnp.dot(a, b, preferred_element_type=F32)


def data_times(x, table):
    high, low = split(x)
    return dot(high, table[0]) + (dot(low, table[0]) + dot(high, table[1]))


def times_data(table, x):
    high, low = split(x)
    return dot(table[0], high) + (dot(table[0], low) + dot(table[1], high))


def projected(get):
    im0, im1, im2 = get(1, 0, 0), get(1, 1, 1), get(1, 2, 2)
    third = (im0 + im1 + im2) * (1.0 / 3.0)
    out = [im0 - third, im1 - third]
    for i, j in ((0, 1), (0, 2), (1, 2)):
        out.append(0.5 * (get(0, i, j) - get(0, j, i)))
        out.append(0.5 * (get(1, i, j) + get(1, j, i)))
    return out


def cayley(a):
    h0, h1, q01, p01, q02, p02, q12, p12 = a
    h2 = -(h0 + h1)
    s01 = p01 * p01 + q01 * q01
    s02 = p02 * p02 + q02 * q02
    s12 = p12 * p12 + q12 * q12
    t0, t1, t2 = h0 * h0, h1 * h1, h2 * h2
    plus = 1.0 + (0.5 * (t0 + t1 + t2) + (s01 + s02 + s12))
    mr = p01 * p12 - q01 * q12
    mi = -(p01 * q12 + q01 * p12)
    nr = p02 * p12 + q02 * q12
    ni = p02 * q12 - q02 * p12
    kr = p01 * p02 + q01 * q02
    ki = q01 * p02 - p01 * q02
    delta = h0 * h1 * h2 + 2.0 * (mr * p02 - mi * q02) - (h0 * s12 + h1 * s02 + h2 * s01)
    scale = 2.0 / (plus * plus + delta * delta)
    u = plus * scale
    v = -delta * scale
    real = [[None] * 3 for _ in range(3)]
    imag = [[None] * 3 for _ in range(3)]
    for i, (h, b) in enumerate(
        (
            (h0, plus - (t0 + s01 + s02)),
            (h1, plus - (t1 + s01 + s12)),
            (h2, plus - (t2 + s02 + s12)),
        )
    ):
        real[i][i] = u * b - v * h - 1.0
        imag[i][i] = u * h + v * b
    for i, j, p, q, br, bi in (
        (0, 1, p01, q01, h2 * p01 - nr, -h2 * q01 - ni),
        (0, 2, p02, q02, h1 * p02 - mr, -h1 * q02 - mi),
        (1, 2, p12, q12, h0 * p12 - kr, -h0 * q12 - ki),
    ):
        ur, ui = br + q, bi + p
        lr, li = br - q, p - bi
        real[i][j] = u * ur - v * ui
        imag[i][j] = u * ui + v * ur
        real[j][i] = u * lr - v * li
        imag[j][i] = u * li + v * lr
    return [real[i][j] for i in range(3) for j in range(3)] + [imag[i][j] for i in range(3) for j in range(3)]


def product(a, b):
    real, imag = [], []
    for i in range(3):
        for j in range(3):
            r = m = None
            for k in range(3):
                ar, ai = a[3 * i + k], a[9 + 3 * i + k]
                br, bi = b[3 * k + j], b[9 + 3 * k + j]
                x, y = ar * br - ai * bi, ar * bi + ai * br
                r, m = (x, y) if r is None else (r + x, m + y)
            real.append(r)
            imag.append(m)
    return real + imag


def product_dagger(a, b):
    real, imag = [], []
    for i in range(3):
        for j in range(3):
            r = m = None
            for k in range(3):
                ar, ai = a[3 * i + k], a[9 + 3 * i + k]
                br, bi = b[3 * j + k], b[9 + 3 * j + k]
                x, y = ar * br + ai * bi, ai * br - ar * bi
                r, m = (x, y) if r is None else (r + x, m + y)
            real.append(r)
            imag.append(m)
    return real + imag


def forward_modes(fields, spread, down, tiles_ref, q):
    part = data_times(fields, spread)
    stacked = jnp.concatenate(
        [
            jnp.concatenate([part[24 * f : 24 * f + 24, 128 * k : 128 * k + 128] for f in range(4)], axis=1)
            for k in range(4)
        ],
        axis=0,
    )
    modes = times_data(down, stacked)
    lane = lax.broadcasted_iota(jnp.int32, (SIDE, 128), 1)
    last = modes[:, 384:]
    for j in range(3):
        tile = jnp.where(lane < 96, modes[:, 128 * j : 128 * j + 128], pltpu.roll(last, 96 - 32 * j, 1))
        for b in range(12):
            tiles_ref[36 * q + 3 * b + j] = tile[8 * b : 8 * b + 8]


def inverse_fields(tiles_ref, spread_t, down_t, halves):
    lane = lax.broadcasted_iota(jnp.int32, (SIDE, 128), 1)
    blocks = []
    for q in halves:
        tiles = [
            jnp.concatenate([tiles_ref[36 * q + 3 * b + j] for b in range(12)], axis=0) for j in range(3)
        ]
        rolled = [pltpu.roll(tiles[j], 32 * j + 32, 1) for j in range(3)]
        last = jnp.where(lane < 32, rolled[0], jnp.where(lane < 64, rolled[1], rolled[2]))
        blocks += tiles + [last]
    stacked = times_data(down_t, jnp.concatenate(blocks, axis=1))
    part = jnp.concatenate(
        [
            jnp.concatenate([stacked[24 * k : 24 * k + 24, 128 * f : 128 * f + 128] for k in range(4)], axis=1)
            for f in range(4 * len(halves))
        ],
        axis=0,
    )
    return data_times(part, spread_t)


def row_turned(x, shift):
    count = x.shape[0] // ROWS
    return pltpu.roll(x.reshape(count, ROWS, x.shape[1]), shift, 1).reshape(x.shape)


def lane_of(x):
    return lax.broadcasted_iota(jnp.int32, x.shape, 1)


def from_y_before(x):
    turned = pltpu.roll(x, 96, 1)
    return jnp.where(lane_of(x) < 96, row_turned(turned, 1), turned)


def from_z_before(x):
    return jnp.where(lane_of(x) % 96 == 0, pltpu.roll(x, LANES - 95, 1), pltpu.roll(x, 1, 1))


def from_y_after(x):
    turned = pltpu.roll(x, LANES - 96, 1)
    return jnp.where(lane_of(x) >= 288, row_turned(turned, ROWS - 1), turned)


def from_z_after(x):
    return jnp.where(lane_of(x) % 96 == 95, pltpu.roll(x, 95, 1), pltpu.roll(x, LANES - 1, 1))


def chips():
    def hops(step):
        return min(step[0], 4 - step[0]) + min(step[1], 8 - step[1])

    steps = [(dx, dy) for dx in range(4) for dy in range(8) if dx or dy]
    return sorted(steps, key=lambda step: (-hops(step), step[1], step[0]))


def kernel(
    u_hbm, spread_hbm, spread_t_hbm, down_hbm, down_t_hbm, along_hbm, plane_hbm, square_hbm,
    out, drift_ref,
    u, spread, spread_t, down, down_t, along, plane, square_x,
    own, prev, rest, snd, rcv, sol, back, ahead, part, parts,
    g, gy, gz, gx, act,
    local_sem, edge_send, edge_recv, onward_send, onward_recv, far_send, far_recv, relay,
):
    me = lax.axis_index("gx")
    x, y, c = me // 16, (me // 2) % 8, me % 2
    after, before = (me + 1) % NX, (me + NX - 1) % NX

    def device(dx, dy, core):
        return ((x + dx) % 4) * 16 + ((y + dy) % 8) * 2 + core

    barrier = pltpu.get_barrier_semaphore()

    def signal(sem, peer):
        pl.semaphore_signal(sem, inc=1, device_id={"gx": peer}, device_id_type=MESH)

    edge_left = jnp.logical_and(y == 0, c == 0)
    edge_right = jnp.logical_and(y == 7, c == 1)
    signal(barrier, device(0, 0, 1 - c))
    for core in range(2):
        for dx, dy in ((0, 1), (0, 7), (1, 0), (3, 0)):
            signal(barrier, device(dx, dy, core))

    @pl.when(edge_left)
    def _():
        signal(barrier, before)

    @pl.when(edge_right)
    def _():
        signal(barrier, after)

    loads = [
        pltpu.make_async_copy(u_hbm.at[pl.ds(18 * d, 18)], u.at[pl.ds(18 * d, 18)], local_sem.at[d])
        for d in range(3)
    ]
    for i, (source, target) in enumerate(
        (
            (spread_hbm, spread), (down_hbm, down), (plane_hbm.at[me], plane), (square_hbm, square_x),
            (along_hbm, along), (down_t_hbm, down_t), (spread_t_hbm, spread_t),
        )
    ):
        loads.append(pltpu.make_async_copy(source, target, local_sem.at[3 + i]))
    for load in loads:
        load.start()

    def project(d, into):
        for j in range(3):
            fields = projected(
                lambda p, a, b: u[18 * d + 9 * p + 3 * a + b, pl.ds(j, ROWS, stride=3), :]
            )
            for f in range(8):
                into[pl.ds(ROWS * f, ROWS), pl.ds(128 * j, 128)] = fields[f]

    loads[0].wait()
    project(0, own)

    pl.semaphore_wait(barrier, 9 + jnp.where(jnp.logical_or(edge_left, edge_right), 1, 0))
    edges = [
        pltpu.make_async_remote_copy(
            src_ref=own.at[pl.ds(96 * q, 96)], dst_ref=prev.at[pl.ds(96 * q, 96)],
            send_sem=edge_send.at[q], recv_sem=edge_recv.at[q],
            device_id={"gx": after}, device_id_type=MESH,
        )
        for q in range(2)
    ]
    for edge in edges:
        edge.start()
    for dx in (1, 3):
        signal(relay.at[0], device(dx, 0, c))

    loads[1].wait()
    project(1, act)
    pl.semaphore_wait(relay.at[0], 2)
    for dy in (1, 7):
        signal(relay.at[1], device(0, dy, c))
    middle = act[...]
    rest[...] = from_y_before(middle) - middle - own[...]
    loads[2].wait()
    project(2, act)
    pl.semaphore_wait(relay.at[1], 2)
    for dx in (0, 1, 3):
        for dy in (2, 6):
            signal(relay.at[2], device(dx, dy, c))
    middle = act[...]
    rest[...] += from_z_before(middle) - middle
    for load in loads[3:]:
        load.wait()

    factor = PEAK_SQUARE * STEP_SIZE * 0.5 / (NX * CELLS)
    filters = []
    for i in range(9):
        square = square_x[...] + plane[pl.ds(i, 1), :]
        positive = square > 0.0
        filters.append(jnp.where(positive, factor / jnp.where(positive, square, 1.0), 0.0))
    filters = jnp.concatenate(filters, axis=1)

    def place(core, chip):
        return pl.ds(36 * core + 9 * (chip // 8), 9), chip % 8

    def there(peer, core):
        return pltpu.make_async_remote_copy(
            src_ref=snd.at[place(core, peer // 2)], dst_ref=rcv.at[:, me],
            send_sem=far_send.at[0], recv_sem=far_recv.at[0],
            device_id={"gx": peer}, device_id_type=MESH,
        )

    partial = None
    for q in range(2):
        edges[q].wait_recv()
        rows = pl.ds(96 * q, 96)
        fields = rest[rows, :] + prev[rows, :]
        tail = fields[48:] if q == 0 else fields
        total = 2.0 * jnp.sum(tail * tail, axis=0, keepdims=True)
        if q == 0:
            f0, f1 = fields[:24], fields[24:48]
            both = f0 + f1
            total += jnp.sum(f0 * f0 + f1 * f1 + both * both, axis=0, keepdims=True)
        partial = total if partial is None else partial + total
        forward_modes(fields, spread, down, snd, q)
        if q == 0:
            pl.semaphore_wait(relay.at[2], 6)
        for dx, dy in chips():
            there(device(dx, dy, q), q).start()

        @pl.when(c != q)
        def _():
            there(device(0, 0, q), q).start()

        @pl.when(c == q)
        def _():
            pltpu.make_async_copy(snd.at[place(q, me // 2)], rcv.at[:, me], far_recv.at[0]).start()

    partial = partial[:, :128] + partial[:, 128:256] + partial[:, 256:]
    part[...] = jnp.broadcast_to(partial, (8, 128))

    def share(k, carry):
        pltpu.make_async_remote_copy(
            src_ref=part.at[0], dst_ref=parts.at[me], send_sem=far_send.at[2], recv_sem=far_recv.at[2],
            device_id={"gx": (me + k) % NX}, device_id_type=MESH,
        ).start()
        return carry

    lax.fori_loop(1, NX, share, 0)
    pltpu.make_async_copy(part.at[0], parts.at[me], far_recv.at[2]).start()

    def arrived(ref, sem):
        pltpu.make_async_copy(ref, ref, sem).wait()

    arrived(rcv, far_recv.at[0])
    waves = times_data(along, jnp.concatenate([rcv[i] for i in range(9)], axis=1))
    waves = times_data(along, waves * filters)
    for i in range(9):
        sol[i] = waves[:, 128 * i : 128 * i + 128]

    tiles, line = place(c, me // 2)
    for dx, dy in chips() + [(0, 0)]:
        for core in range(2):
            peer = device(dx, dy, core if dx or dy else 1 - c)
            if not (dx or dy) and core:
                continue
            pltpu.make_async_remote_copy(
                src_ref=sol.at[:, peer], dst_ref=back.at[tiles, line],
                send_sem=far_send.at[1], recv_sem=far_recv.at[1],
                device_id={"gx": peer}, device_id_type=MESH,
            ).start()
    pltpu.make_async_copy(sol.at[:, me], back.at[tiles, line], far_recv.at[1]).start()

    arrived(parts, far_recv.at[2])
    drift_ref[0] = jnp.sum(parts[...]) * (1.0 / (9.0 * NX * CELLS))
    arrived(rcv.at[:, pl.ds(0, NX - 1)], far_send.at[0])
    arrived(parts.at[pl.ds(0, NX - 1)], far_send.at[2])
    for edge in edges:
        edge.wait_send()

    arrived(back, far_recv.at[1])
    onward = [
        pltpu.make_async_remote_copy(
            src_ref=back.at[pl.ds(36 * q, 36)], dst_ref=ahead.at[pl.ds(36 * q, 36)],
            send_sem=onward_send.at[q], recv_sem=onward_recv.at[q],
            device_id={"gx": before}, device_id_type=MESH,
        )
        for q in range(2)
    ]
    for half in onward:
        half.start()

    def chunks(action):
        def body(k, carry):
            i, t = k // 3, k % 3
            r, j = pl.multiple_of(8 * i, 8), pl.multiple_of(128 * t, 128)
            action(
                lambda ref, count: [ref[pl.ds(ROWS * e + r, 8), pl.ds(j, 128)] for e in range(count)],
                lambda ref, e: (ROWS * e + r, j),
                pl.ds(24 * i + t, 8, stride=3),
            )
            return carry

        lax.fori_loop(0, 9, body, 0)

    def rotate(into):
        def action(read, at, sites):
            entries = cayley(read(act, 8))
            for e in range(18):
                r, j = at(into, e)
                into[pl.ds(r, 8), pl.ds(j, 128)] = entries[e]

        chunks(action)

    act[...] = inverse_fields(back, spread_t, down_t, (0, 1))
    rotate(g)
    whole = g[...]
    gy[...] = from_y_after(whole)
    gz[...] = from_z_after(whole)

    def update(read, at, sites):
        left = read(g, 18)
        for d, aheads in ((1, gy), (2, gz)):
            links = [u[18 * d + e, sites, :] for e in range(18)]
            new = product_dagger(product(left, links), read(aheads, 18))
            for e in range(18):
                out[18 * d + e, sites, :] = new[e]
        new = product(left, [u[e, sites, :] for e in range(18)])
        for e in range(18):
            r, j = at(gx, e)
            gx[pl.ds(r, 8), pl.ds(j, 128)] = new[e]

    chunks(update)

    for q in range(2):
        onward[q].wait_recv()
        act[pl.ds(96 * q, 96), :] = inverse_fields(ahead, spread_t, down_t, (q,))

    def finish(read, at, sites):
        new = product_dagger(read(gx, 18), cayley(read(act, 8)))
        for e in range(18):
            out[e, sites, :] = new[e]

    chunks(finish)
    arrived(rcv.at[:, pl.ds(0, NX - 1)], far_send.at[1])
    for half in onward:
        half.wait_send()


def local(gauge_links):
    tables = [jnp.asarray(t) for t in make_tables()]
    hbm = pl.BlockSpec(memory_space=pltpu.HBM)
    dma = pltpu.SemaphoreType.DMA
    fields = pltpu.VMEM((8 * ROWS, LANES), F32)
    matrix = pltpu.VMEM((18 * ROWS, LANES), F32)
    tiles = pltpu.VMEM((72, 8, 128), F32)
    waves = pltpu.VMEM((9, NX, 128), F32)
    links, drift = pl.pallas_call(
        kernel,
        out_shape=(
            pltpu.VMEM((54, 72, 128), F32),
            jax.ShapeDtypeStruct((1,), F32),
        ),
        in_specs=[hbm] * 8,
        out_specs=(pl.BlockSpec(memory_space=pltpu.VMEM), pl.BlockSpec(memory_space=pltpu.SMEM)),
        scratch_shapes=[
            pltpu.VMEM((54, 72, 128), F32),
            pltpu.VMEM((2, LANES, 512), BF16),
            pltpu.VMEM((2, 512, LANES), BF16),
            pltpu.VMEM((2, SIDE, SIDE), BF16),
            pltpu.VMEM((2, SIDE, SIDE), BF16),
            pltpu.VMEM((2, NX, NX), BF16),
            pltpu.VMEM((9, 128), F32),
            pltpu.VMEM((NX, 128), F32),
            fields, fields, fields,
            tiles, waves, waves, tiles, tiles,
            pltpu.VMEM((8, 128), F32),
            pltpu.VMEM((NX, 128), F32),
            matrix, matrix, matrix, matrix,
            fields,
            dma((10,)), dma((2,)), dma((2,)), dma((2,)), dma((2,)), dma((3,)), dma((3,)),
            pltpu.SemaphoreType.REGULAR((3,)),
        ],
        compiler_params=pltpu.CompilerParams(
            collective_id=0, has_side_effects=True, vmem_limit_bytes=24 << 20
        ),
    )(*[pltpu.with_memory_space_constraint(t, pltpu.HBM) for t in (gauge_links.reshape(54, 72, 128), *tables)])
    return links.reshape(gauge_links.shape), drift


def solution(mesh):
    split_x = ("ta", "gx")
    return jax.shard_map(
        local,
        mesh=mesh,
        in_specs=(P(None, None, None, None, split_x, None),),
        out_specs=(P(None, None, None, None, split_x, None), P("ta")),
        check_vma=False,
    )
```

time: 55 us -> 44 us (0.80)
  Pallas kernels: 49.4 us -> 40.3 us
  local copies, waits for them, and re-layouts: 2.96 us -> 1.28 us
    pallas_call x1, Pallas kernels: 49.4 us -> 40.3 us  [local(): pl.pallas_call(kernel, out_shape=(pltpu.VMEM((54, 72, 128), F32), jax.Sha...]
    unnamed x1, local copies, waits for them, and re-layouts: 2.96 us -> 1.28 us
where the time goes in v1:
time: 44 us; the launch traced here: 43.9 us
  Pallas kernels  40.3 us (92%)
  between operations  2.33 us (5%)
  local copies, waits for them, and re-layouts  1.28 us (3%)
    pallas_call x1, Pallas kernels, local(): pl.pallas_call(kernel, out_shape=(pltpu.VMEM((54, 72, 128), F32), jax.Sha...  40.3 us
    unnamed x1, local copies, waits for them, and re-layouts  1.28 us

profile of v1, /device:TPU:1, one launch (start us, length us, event | category | flops | bytes accessed | tf_op | source)
XLA Modules:
  0.0 43.9 jit_solution(15029406899861635427)
XLA Ops:
  0.6 40.3 %shard_map.95 = (f32[54,72,128]{2,1,0:T(8,128)S(1)}, f32[1]{0:T(128)}) custom-call(f32[54,72,128]{2,1,0:T(8,128)} %bitcast.3, bf16[2,384,512]{2,1,0:T(8,128)(2,1)} %constant.14.clone.spread_hbm, bf16[2,512,384]{2,1,0:T(8,128)(2,1)} %constant.15.clone.spread_t_hbm, bf16[2,96,96]{2,1,0:T(8,128)(2,1)} %constant.16.clone.down_hbm, ...), custom_call_target="tpu_custom_call" | custom-call | tf_op jit(solution)/shard_map/pallas_call | solution.py:499
  40.9 1.3 %copy.14 = f32[3,2,3,3,1,9216]{5,4,3,2,1,0:T(1,128)} copy(f32[3,2,3,3,1,9216]{5,4,3,2,1,0:T(1,128)S(1)} %bitcast.2) | data formatting | bytes 3981312

commit v2 on v1

--- a/solution.py
+++ b/solution.py
@@ -57,9 +57,9 @@
     return (
         halves(spread),
         halves(spread.T),
-        halves(down),
-        halves(down.T),
-        halves(cas(NX)),
+        halves(down).reshape(2 * SIDE, SIDE),
+        halves(down.T).reshape(2 * SIDE, SIDE),
+        halves(cas(NX)).reshape(2 * NX, NX),
         plane,
         np.ascontiguousarray(along),
     )
@@ -76,12 +76,16 @@
 
 def data_times(x, table):
     high, low = split(x)
-    return dot(high, table[0]) + (dot(low, table[0]) + dot(high, table[1]))
+    rows = x.shape[0]
+    both = dot(jnp.concatenate([high, low], axis=0), table[0])
+    return both[:rows] + (both[rows:] + dot(high, table[1]))
 
 
 def times_data(table, x):
     high, low = split(x)
-    return dot(table[0], high) + (dot(table[0], low) + dot(table[1], high))
+    rows = table.shape[0] // 2
+    both = dot(table[...], high)
+    return both[:rows] + (both[rows:] + dot(table[:rows], low))
 
 
 def projected(get):
@@ -217,7 +221,9 @@
 
 def from_y_before(x):
     turned = pltpu.roll(x, 96, 1)
-    return jnp.where(lane_of(x) < 96, row_turned(turned, 1), turned)
+    first = turned[:, :128]
+    first = jnp.where(lane_of(first) < 96, row_turned(first, 1), first)
+    return jnp.concatenate([first, turned[:, 128:]], axis=1)
 
 
 def from_z_before(x):
@@ -226,7 +232,9 @@
 
 def from_y_after(x):
     turned = pltpu.roll(x, LANES - 96, 1)
-    return jnp.where(lane_of(x) >= 288, row_turned(turned, ROWS - 1), turned)
+    last = turned[:, 256:]
+    last = jnp.where(lane_of(last) >= 32, row_turned(last, ROWS - 1), last)
+    return jnp.concatenate([turned[:, :256], last], axis=1)
 
 
 def from_z_after(x):
@@ -239,13 +247,17 @@
 
     steps = [(dx, dy) for dx in range(4) for dy in range(8) if dx or dy]
     return sorted(steps, key=lambda step: (-hops(step), step[1], step[0]))
+
+
+EARLY = ((4,), (3, 5), (2, 6))
+LATE = (0, 1, 7)
 
 
 def kernel(
     u_hbm, spread_hbm, spread_t_hbm, down_hbm, down_t_hbm, along_hbm, plane_hbm, square_hbm,
     out, drift_ref,
     u, spread, spread_t, down, down_t, along, plane, square_x,
-    own, prev, rest, snd, rcv, sol, back, ahead, part, parts,
+    own, prev, rest, snd, rcv, sol, back, ahead, part, parts, total_ref,
     g, gy, gz, gx, act,
     local_sem, edge_send, edge_recv, onward_send, onward_recv, far_send, far_recv, relay,
 ):
@@ -260,21 +272,6 @@
 
     def signal(sem, peer):
         pl.semaphore_signal(sem, inc=1, device_id={"gx": peer}, device_id_type=MESH)
-
-    edge_left = jnp.logical_and(y == 0, c == 0)
-    edge_right = jnp.logical_and(y == 7, c == 1)
-    signal(barrier, device(0, 0, 1 - c))
-    for core in range(2):
-        for dx, dy in ((0, 1), (0, 7), (1, 0), (3, 0)):
-            signal(barrier, device(dx, dy, core))
-
-    @pl.when(edge_left)
-    def _():
-        signal(barrier, before)
-
-    @pl.when(edge_right)
-    def _():
-        signal(barrier, after)
 
     loads = [
         pltpu.make_async_copy(u_hbm.at[pl.ds(18 * d, 18)], u.at[pl.ds(18 * d, 18)], local_sem.at[d])
@@ -287,7 +284,24 @@
         )
     ):
         loads.append(pltpu.make_async_copy(source, target, local_sem.at[3 + i]))
-    for load in loads:
+    loads[0].start()
+
+    edge_left = jnp.logical_and(y == 0, c == 0)
+    edge_right = jnp.logical_and(y == 7, c == 1)
+    signal(barrier, device(0, 0, 1 - c))
+    for core in range(2):
+        for dx, dy in ((0, 1), (0, 7), (1, 0), (3, 0)):
+            signal(barrier, device(dx, dy, core))
+
+    @pl.when(edge_left)
+    def _():
+        signal(barrier, before)
+
+    @pl.when(edge_right)
+    def _():
+        signal(barrier, after)
+
+    for load in loads[1:]:
         load.start()
 
     def project(d, into):
@@ -298,10 +312,12 @@
             for f in range(8):
                 into[pl.ds(ROWS * f, ROWS), pl.ds(128 * j, 128)] = fields[f]
 
+    def entered():
+        pl.semaphore_wait(barrier, 9 + jnp.where(jnp.logical_or(edge_left, edge_right), 1, 0))
+
     loads[0].wait()
     project(0, own)
-
-    pl.semaphore_wait(barrier, 9 + jnp.where(jnp.logical_or(edge_left, edge_right), 1, 0))
+    entered()
     edges = [
         pltpu.make_async_remote_copy(
             src_ref=own.at[pl.ds(96 * q, 96)], dst_ref=prev.at[pl.ds(96 * q, 96)],
@@ -314,20 +330,20 @@
         edge.start()
     for dx in (1, 3):
         signal(relay.at[0], device(dx, 0, c))
-
-    loads[1].wait()
-    project(1, act)
     pl.semaphore_wait(relay.at[0], 2)
     for dy in (1, 7):
         signal(relay.at[1], device(0, dy, c))
+    pl.semaphore_wait(relay.at[1], 2)
+    for dx in (0, 1, 3):
+        for dy in (2, 6):
+            signal(relay.at[2], device(dx, dy, c))
+
+    loads[1].wait()
+    project(1, act)
     middle = act[...]
     rest[...] = from_y_before(middle) - middle - own[...]
     loads[2].wait()
     project(2, act)
-    pl.semaphore_wait(relay.at[1], 2)
-    for dx in (0, 1, 3):
-        for dy in (2, 6):
-            signal(relay.at[2], device(dx, dy, c))
     middle = act[...]
     rest[...] += from_z_before(middle) - middle
     for load in loads[3:]:
@@ -350,6 +366,9 @@
             send_sem=far_send.at[0], recv_sem=far_recv.at[0],
             device_id={"gx": peer}, device_id_type=MESH,
         )
+
+    def arrived(ref, sem):
+        pltpu.make_async_copy(ref, ref, sem).wait()
 
     partial = None
     for q in range(2):
@@ -378,20 +397,21 @@
             pltpu.make_async_copy(snd.at[place(q, me // 2)], rcv.at[:, me], far_recv.at[0]).start()
 
     partial = partial[:, :128] + partial[:, 128:256] + partial[:, 256:]
-    part[...] = jnp.broadcast_to(partial, (8, 128))
-
-    def share(k, carry):
-        pltpu.make_async_remote_copy(
-            src_ref=part.at[0], dst_ref=parts.at[me], send_sem=far_send.at[2], recv_sem=far_recv.at[2],
-            device_id={"gx": (me + k) % NX}, device_id_type=MESH,
+    part[0] = jnp.broadcast_to(partial, (8, 128))
+
+    def share(stage, row, peers):
+        for peer in peers:
+            pltpu.make_async_remote_copy(
+                src_ref=part.at[stage], dst_ref=parts.at[stage, row],
+                send_sem=far_send.at[2 + stage], recv_sem=far_recv.at[2 if stage == 0 else 6],
+                device_id={"gx": peer}, device_id_type=MESH,
+            ).start()
+        pltpu.make_async_copy(
+            part.at[stage], parts.at[stage, row], far_recv.at[2 if stage == 0 else 6]
         ).start()
-        return carry
-
-    lax.fori_loop(1, NX, share, 0)
-    pltpu.make_async_copy(part.at[0], parts.at[me], far_recv.at[2]).start()
-
-    def arrived(ref, sem):
-        pltpu.make_async_copy(ref, ref, sem).wait()
+
+    share(0, y, [device(0, dy, c) for dy in range(1, 8)])
+
 
     arrived(rcv, far_recv.at[0])
     waves = times_data(along, jnp.concatenate([rcv[i] for i in range(9)], axis=1))
@@ -400,6 +420,7 @@
         sol[i] = waves[:, 128 * i : 128 * i + 128]
 
     tiles, line = place(c, me // 2)
+    came = {dy: 3 + i for i, group in enumerate(EARLY) for dy in group}
     for dx, dy in chips() + [(0, 0)]:
         for core in range(2):
             peer = device(dx, dy, core if dx or dy else 1 - c)
@@ -407,29 +428,35 @@
                 continue
             pltpu.make_async_remote_copy(
                 src_ref=sol.at[:, peer], dst_ref=back.at[tiles, line],
-                send_sem=far_send.at[1], recv_sem=far_recv.at[1],
+                send_sem=far_send.at[1], recv_sem=far_recv.at[1 if dy in LATE else came[dy]],
                 device_id={"gx": peer}, device_id_type=MESH,
             ).start()
     pltpu.make_async_copy(sol.at[:, me], back.at[tiles, line], far_recv.at[1]).start()
 
-    arrived(parts, far_recv.at[2])
-    drift_ref[0] = jnp.sum(parts[...]) * (1.0 / (9.0 * NX * CELLS))
+    arrived(parts.at[0], far_recv.at[2])
+    part[1] = jnp.broadcast_to(jnp.sum(parts[0, :, 0, :], axis=0, keepdims=True), (8, 128))
+    share(1, 2 * x + c, [device(dx, 0, core) for dx in range(1, 4) for core in range(2)] + [device(0, 0, 1 - c)])
     arrived(rcv.at[:, pl.ds(0, NX - 1)], far_send.at[0])
-    arrived(parts.at[pl.ds(0, NX - 1)], far_send.at[2])
+    arrived(parts.at[0, pl.ds(0, 7)], far_send.at[2])
     for edge in edges:
         edge.wait_send()
 
-    arrived(back, far_recv.at[1])
-    onward = [
+    def onward(part, dy, sem):
+        rows = (part, (y + dy) % 8)
         pltpu.make_async_remote_copy(
-            src_ref=back.at[pl.ds(36 * q, 36)], dst_ref=ahead.at[pl.ds(36 * q, 36)],
-            send_sem=onward_send.at[q], recv_sem=onward_recv.at[q],
+            src_ref=back.at[rows], dst_ref=ahead.at[rows],
+            send_sem=onward_send.at[0], recv_sem=onward_recv.at[sem],
             device_id={"gx": before}, device_id_type=MESH,
-        )
-        for q in range(2)
-    ]
-    for half in onward:
-        half.start()
+        ).start()
+
+    for i, group in enumerate(EARLY):
+        arrived(back.at[pl.ds(0, 9 * len(group))], far_recv.at[3 + i])
+        for dy in group:
+            onward(pl.ds(0, 72), dy, 0)
+    arrived(back.at[pl.ds(0, 9 * len(LATE))], far_recv.at[1])
+    for q in range(2):
+        for dy in LATE:
+            onward(pl.ds(36 * q, 36), dy, 1 + q)
 
     def chunks(action):
         def body(k, carry):
@@ -473,8 +500,14 @@
 
     chunks(update)
 
+    arrived(ahead.at[pl.ds(0, 72 - 9 * len(LATE))], onward_recv.at[0])
+    arrived(parts.at[1], far_recv.at[6])
+    total_ref[0] = jnp.sum(parts[1, :, 0, :]) * (1.0 / (9.0 * NX * CELLS))
+    drift = pltpu.make_async_copy(total_ref, drift_ref, local_sem.at[0])
+    drift.start()
+
     for q in range(2):
-        onward[q].wait_recv()
+        arrived(snd.at[pl.ds(0, 36), pl.ds(0, len(LATE))], onward_recv.at[1 + q])
         act[pl.ds(96 * q, 96), :] = inverse_fields(ahead, spread_t, down_t, (q,))
 
     def finish(read, at, sites):
@@ -484,8 +517,9 @@
 
     chunks(finish)
     arrived(rcv.at[:, pl.ds(0, NX - 1)], far_send.at[1])
-    for half in onward:
-        half.wait_send()
+    arrived(parts.at[0, pl.ds(0, 7)], far_send.at[3])
+    drift.wait()
+    arrived(back, onward_send.at[0])
 
 
 def local(gauge_links):
@@ -503,23 +537,24 @@
             jax.ShapeDtypeStruct((1,), F32),
         ),
         in_specs=[hbm] * 8,
-        out_specs=(pl.BlockSpec(memory_space=pltpu.VMEM), pl.BlockSpec(memory_space=pltpu.SMEM)),
+        out_specs=(pl.BlockSpec(memory_space=pltpu.VMEM), pl.BlockSpec(memory_space=pl.ANY)),
         scratch_shapes=[
             pltpu.VMEM((54, 72, 128), F32),
             pltpu.VMEM((2, LANES, 512), BF16),
             pltpu.VMEM((2, 512, LANES), BF16),
-            pltpu.VMEM((2, SIDE, SIDE), BF16),
-            pltpu.VMEM((2, SIDE, SIDE), BF16),
-            pltpu.VMEM((2, NX, NX), BF16),
+            pltpu.VMEM((2 * SIDE, SIDE), BF16),
+            pltpu.VMEM((2 * SIDE, SIDE), BF16),
+            pltpu.VMEM((2 * NX, NX), BF16),
             pltpu.VMEM((9, 128), F32),
             pltpu.VMEM((NX, 128), F32),
             fields, fields, fields,
             tiles, waves, waves, tiles, tiles,
-            pltpu.VMEM((8, 128), F32),
-            pltpu.VMEM((NX, 128), F32),
+            pltpu.VMEM((2, 8, 128), F32),
+            pltpu.VMEM((2, 8, 8, 128), F32),
+            pltpu.SMEM((1,), F32),
             matrix, matrix, matrix, matrix,
             fields,
-            dma((10,)), dma((2,)), dma((2,)), dma((2,)), dma((2,)), dma((3,)), dma((3,)),
+            dma((10,)), dma((2,)), dma((2,)), dma((1,)), dma((3,)), dma((4,)), dma((7,)),
             pltpu.SemaphoreType.REGULAR((3,)),
         ],
         compiler_params=pltpu.CompilerParams(

time: 44 us -> 42.3 us (0.961)
  Pallas kernels: 40.3 us -> 38.6 us
    pallas_call x1, Pallas kernels: 40.3 us -> 38.6 us  [local(): pl.pallas_call(kernel, out_shape=(pltpu.VMEM((54, 72, 128), F32), jax.Sha...]
where the time goes in v2:
time: 42.3 us; the launch traced here: 42.2 us
  Pallas kernels  38.6 us (91%)
  between operations  2.33 us (6%)
  local copies, waits for them, and re-layouts  1.28 us (3%)
    pallas_call x1, Pallas kernels, local(): pl.pallas_call(kernel, out_shape=(pltpu.VMEM((54, 72, 128), F32), jax.Sha...  38.6 us
    unnamed x1, local copies, waits for them, and re-layouts  1.28 us

profile of v2, /device:TPU:1, one launch (start us, length us, event | category | flops | bytes accessed | tf_op | source)
XLA Modules:
  0.0 42.2 jit_solution(8920367438781785)
XLA Ops:
  0.6 38.6 %shard_map.95 = (f32[54,72,128]{2,1,0:T(8,128)S(1)}, f32[1]{0:T(128)}) custom-call(f32[54,72,128]{2,1,0:T(8,128)} %bitcast.3, bf16[2,384,512]{2,1,0:T(8,128)(2,1)} %constant.14.clone.spread_hbm, bf16[2,512,384]{2,1,0:T(8,128)(2,1)} %constant.15.clone.spread_t_hbm, bf16[192,96]{1,0:T(8,128)(2,1)} %constant.16.clone.down_hbm, ...), custom_call_target="tpu_custom_call" | custom-call | tf_op jit(solution)/shard_map/pallas_call | solution.py:533
  39.2 1.3 %copy.14 = f32[3,2,3,3,1,9216]{5,4,3,2,1,0:T(1,128)} copy(f32[3,2,3,3,1,9216]{5,4,3,2,1,0:T(1,128)S(1)} %bitcast.2) | data formatting | bytes 3981312

commit v3 on v2

--- a/solution.py
+++ b/solution.py
@@ -249,7 +249,7 @@
     return sorted(steps, key=lambda step: (-hops(step), step[1], step[0]))
 
 
-EARLY = ((4,), (3, 5), (2, 6))
+EARLY = (2, 3, 4, 5, 6)
 LATE = (0, 1, 7)
 
 
@@ -284,23 +284,22 @@
         )
     ):
         loads.append(pltpu.make_async_copy(source, target, local_sem.at[3 + i]))
-    loads[0].start()
-
     edge_left = jnp.logical_and(y == 0, c == 0)
     edge_right = jnp.logical_and(y == 7, c == 1)
+    @pl.when(edge_left)
+    def _():
+        signal(barrier, before)
+
+    @pl.when(edge_right)
+    def _():
+        signal(barrier, after)
+
     signal(barrier, device(0, 0, 1 - c))
     for core in range(2):
         for dx, dy in ((0, 1), (0, 7), (1, 0), (3, 0)):
             signal(barrier, device(dx, dy, core))
 
-    @pl.when(edge_left)
-    def _():
-        signal(barrier, before)
-
-    @pl.when(edge_right)
-    def _():
-        signal(barrier, after)
-
+    loads[0].start()
     for load in loads[1:]:
         load.start()
 
@@ -420,7 +419,9 @@
         sol[i] = waves[:, 128 * i : 128 * i + 128]
 
     tiles, line = place(c, me // 2)
-    came = {dy: 3 + i for i, group in enumerate(EARLY) for dy in group}
+    def came(dy):
+        return jnp.where(c == 0, 1, 3 + (dy in LATE))
+
     for dx, dy in chips() + [(0, 0)]:
         for core in range(2):
             peer = device(dx, dy, core if dx or dy else 1 - c)
@@ -428,10 +429,10 @@
                 continue
             pltpu.make_async_remote_copy(
                 src_ref=sol.at[:, peer], dst_ref=back.at[tiles, line],
-                send_sem=far_send.at[1], recv_sem=far_recv.at[1 if dy in LATE else came[dy]],
+                send_sem=far_send.at[1], recv_sem=far_recv.at[came(dy)],
                 device_id={"gx": peer}, device_id_type=MESH,
             ).start()
-    pltpu.make_async_copy(sol.at[:, me], back.at[tiles, line], far_recv.at[1]).start()
+    pltpu.make_async_copy(sol.at[:, me], back.at[tiles, line], far_recv.at[came(0)]).start()
 
     arrived(parts.at[0], far_recv.at[2])
     part[1] = jnp.broadcast_to(jnp.sum(parts[0, :, 0, :], axis=0, keepdims=True), (8, 128))
@@ -441,22 +442,26 @@
     for edge in edges:
         edge.wait_send()
 
-    def onward(part, dy, sem):
-        rows = (part, (y + dy) % 8)
+    def onward(rows, sem):
         pltpu.make_async_remote_copy(
             src_ref=back.at[rows], dst_ref=ahead.at[rows],
             send_sem=onward_send.at[0], recv_sem=onward_recv.at[sem],
             device_id={"gx": before}, device_id_type=MESH,
         ).start()
 
-    for i, group in enumerate(EARLY):
-        arrived(back.at[pl.ds(0, 9 * len(group))], far_recv.at[3 + i])
+    first, second = pl.ds(0, 36), pl.ds(36, 36)
+
+    def inverse(tiles, q):
+        act[pl.ds(96 * q, 96), :] = inverse_fields(tiles, spread_t, down_t, (q,))
+
+    arrived(back.at[first], far_recv.at[1])
+    onward(first, 0)
+    inverse(back, 0)
+    for sem, group in ((3, EARLY), (4, LATE)):
+        arrived(snd.at[pl.ds(0, 36), pl.ds(0, len(group))], far_recv.at[sem])
         for dy in group:
-            onward(pl.ds(0, 72), dy, 0)
-    arrived(back.at[pl.ds(0, 9 * len(LATE))], far_recv.at[1])
-    for q in range(2):
-        for dy in LATE:
-            onward(pl.ds(36 * q, 36), dy, 1 + q)
+            onward((second, (y + dy) % 8), 1)
+    inverse(back, 1)
 
     def chunks(action):
         def body(k, carry):
@@ -480,7 +485,6 @@
 
         chunks(action)
 
-    act[...] = inverse_fields(back, spread_t, down_t, (0, 1))
     rotate(g)
     whole = g[...]
     gy[...] = from_y_after(whole)
@@ -500,15 +504,14 @@
 
     chunks(update)
 
-    arrived(ahead.at[pl.ds(0, 72 - 9 * len(LATE))], onward_recv.at[0])
     arrived(parts.at[1], far_recv.at[6])
     total_ref[0] = jnp.sum(parts[1, :, 0, :]) * (1.0 / (9.0 * NX * CELLS))
     drift = pltpu.make_async_copy(total_ref, drift_ref, local_sem.at[0])
     drift.start()
 
     for q in range(2):
-        arrived(snd.at[pl.ds(0, 36), pl.ds(0, len(LATE))], onward_recv.at[1 + q])
-        act[pl.ds(96 * q, 96), :] = inverse_fields(ahead, spread_t, down_t, (q,))
+        arrived(ahead.at[first], onward_recv.at[q])
+        inverse(ahead, q)
 
     def finish(read, at, sites):
         new = product_dagger(read(gx, 18), cayley(read(act, 8)))

time: 42.3 us -> 41.9 us (level)
  no operation moved by 1% of the time
where the time goes in v3:
time: 41.9 us; the launch traced here: 41.8 us
  Pallas kernels  38.2 us (91%)
  between operations  2.33 us (6%)
  local copies, waits for them, and re-layouts  1.28 us (3%)
    pallas_call x1, Pallas kernels, local(): pl.pallas_call(kernel, out_shape=(pltpu.VMEM((54, 72, 128), F32), jax.Sha...  38.2 us
    unnamed x1, local copies, waits for them, and re-layouts  1.28 us

profile of v3, /device:TPU:1, one launch (start us, length us, event | category | flops | bytes accessed | tf_op | source)
XLA Modules:
  0.0 41.8 jit_solution(17131691073432611242)
XLA Ops:
  0.6 38.2 %shard_map.95 = (f32[54,72,128]{2,1,0:T(8,128)S(1)}, f32[1]{0:T(128)}) custom-call(f32[54,72,128]{2,1,0:T(8,128)} %bitcast.3, bf16[2,384,512]{2,1,0:T(8,128)(2,1)} %constant.14.clone.spread_hbm, bf16[2,512,384]{2,1,0:T(8,128)(2,1)} %constant.15.clone.spread_t_hbm, bf16[192,96]{1,0:T(8,128)(2,1)} %constant.16.clone.down_hbm, ...), custom_call_target="tpu_custom_call" | custom-call | tf_op jit(solution)/shard_map/pallas_call | solution.py:536
  38.8 1.3 %copy.14 = f32[3,2,3,3,1,9216]{5,4,3,2,1,0:T(1,128)} copy(f32[3,2,3,3,1,9216]{5,4,3,2,1,0:T(1,128)S(1)} %bitcast.2) | data formatting | bytes 3981312
